TPU v7x, 256 devices: a whole 4x4x8 slice. The times are simulated.
256 devices in a mesh: tok: 64 (over z, y, core), kv: 4 (over x).
Axes of the slice: x: 4, y: 4, z: 8, core: 2. Of those that a mesh axis runs over, the one named last changes fastest.
Arguments:
- tokens: bfloat16 [16384, 8192], P('tok', 'kv'), may hold values from -6 to 6
- frozen_query: bfloat16 [16384, 8192], P('tok', 'kv')
- trained_keys: bfloat16 [16384, 1024], P('tok', 'kv')
- trained_values: bfloat16 [16384, 1024], P('tok', 'kv'), may hold values from -6 to 6
- frozen_output: bfloat16 [16384, 8192], P('tok', 'kv'), may hold values from -3 to 3
- prompt_key_cache: bfloat16 [2, 256, 1024], P(None, 'kv'), may hold values from -6 to 6
- prompt_value_cache: bfloat16 [2, 256, 1024], P(None, 'kv'), may hold values from -6 to 6
- adapter_down: bfloat16 [256, 64, 8192], P('tok', None, 'kv'), may hold values from -0.0625 to 0.0625
- adapter_up: bfloat16 [256, 64, 8192], P('tok', None, 'kv'), may hold values from -0.75 to 0.75
- row_adapter_index: int32 [2048], replicated, may hold values from 0 to 255, as said below
- row_forget_flag: int32 [2048], replicated, may hold values 0 or 1
- row_prompt_index: int32 [2048], replicated, may hold values from 0 to 1
- row_prompt_length: int32 [2048], replicated, may hold values from 32 to 256, as said below
Outputs:
- grad_down: bfloat16 [256, 64, 8192], P('tok', None, 'kv')
- grad_up: bfloat16 [256, 64, 8192], P('tok', None, 'kv')
Inputs may be any that keep to these rules, and one draw needn't show every extreme that they name: `row_adapter_index`: adapter a is held by index a // 4 of tok, its owner. Among the rows of one index of tok (rows i * 32 to i * 32 + 31) at most 2 name adapters of one owner, and this bound is reached. `row_prompt_length`: every index of tok holds a row of length 256.
All inputs are finite; a program needn't handle non-finite values.
Results may differ from a plain program's by a relative error of at most 0.03.
Values may be sent and summed in bfloat16 or wider, within the bound.
No kernel may reach another device: no remote copies, remote signals or barrier semaphores. Data moves between devices by JAX's collectives and lax.ppermute only.
A program may use at most 128 MiB of HBM per device.

v0:
```python
import math

import jax
import jax.numpy as jnp
from jax import lax
from jax.sharding import PartitionSpec as P

QUERY_HEADS = 64
KEY_HEADS = 8
HEAD_WIDTH = 128
ADAPTER_RANK = 64
QUERY_LENGTH = 8


ADAPTER_SCALE = 0.5


def slot_ranks(owners):
    row_count = owners.shape[-1]
    same_owner = owners[..., :, None] == owners[..., None, :]
    earlier = (
        jnp.arange(row_count, dtype=jnp.int32)[:, None]
        > jnp.arange(row_count, dtype=jnp.int32)[None, :]
    )
    return jnp.sum((same_owner & earlier).astype(jnp.int32), axis=-1)


def route_rows(selector, source):
    flat_source = source.reshape(selector.shape[1], -1)
    return jnp.dot(selector, flat_source, preferred_element_type=jnp.float32).astype(jnp.bfloat16)


def attend_block(
    query_rows,
    own_keys,
    own_values,
    base_rows,
    row_loss_weight,
    row_len,
    row_prompt,
    shared_keys,
    shared_values,
    key_prompt,
    key_place,
):
    answer_len = query_rows.shape[1]
    inv_root = 1.0 / math.sqrt(query_rows.shape[-1])
    shared_scores = (
        jnp.einsum("rqkgd,pkd->rkgqp", query_rows, shared_keys, preferred_element_type=jnp.float32)
        * inv_root
    )
    own_scores = (
        jnp.einsum("rqkgd,rjkd->rkgqj", query_rows, own_keys, preferred_element_type=jnp.float32)
        * inv_root
    )
    shared_seen = (
        (key_prompt[None, :] == row_prompt[:, None]) & (key_place[None, :] < row_len[:, None])
    )[:, None, None, None, :]
    answer_pos = jnp.arange(answer_len, dtype=jnp.int32)
    own_seen = (answer_pos[None, :] <= answer_pos[:, None])[None, None, None, :, :]
    shared_masked = jnp.where(shared_seen, shared_scores, -1e30)
    own_masked = jnp.where(own_seen, own_scores, -1e30)
    row_max = jnp.maximum(
        jnp.max(shared_masked, axis=-1, keepdims=True), jnp.max(own_masked, axis=-1, keepdims=True)
    )
    shared_exp = jnp.where(shared_seen, jnp.exp(shared_masked - row_max), 0.0)
    own_exp = jnp.where(own_seen, jnp.exp(own_masked - row_max), 0.0)
    row_total = jnp.sum(shared_exp, axis=-1, keepdims=True) + jnp.sum(
        own_exp, axis=-1, keepdims=True
    )
    shared_probs = shared_exp / row_total
    own_probs = own_exp / row_total
    attn_out = jnp.einsum(
        "rkgqp,pkd->rqkgd",
        shared_probs.astype(jnp.bfloat16),
        shared_values,
        preferred_element_type=jnp.float32,
    ) + jnp.einsum(
        "rkgqj,rjkd->rqkgd",
        own_probs.astype(jnp.bfloat16),
        own_values,
        preferred_element_type=jnp.float32,
    )
    grad_out = (
        row_loss_weight[:, None, None, None, None] * (attn_out - base_rows.astype(jnp.float32))
    ).astype(jnp.bfloat16)
    shared_grad = jnp.einsum(
        "rqkgd,pkd->rkgqp", grad_out, shared_values, preferred_element_type=jnp.float32
    )
    own_grad = jnp.einsum(
        "rqkgd,rjkd->rkgqj", grad_out, own_values, preferred_element_type=jnp.float32
    )
    inner_sum = jnp.sum(shared_probs * shared_grad, axis=-1, keepdims=True) + jnp.sum(
        own_probs * own_grad, axis=-1, keepdims=True
    )
    shared_gscore = (shared_probs * (shared_grad - inner_sum) * inv_root).astype(jnp.bfloat16)
    own_gscore = (own_probs * (own_grad - inner_sum) * inv_root).astype(jnp.bfloat16)
    query_gradient = jnp.einsum(
        "rkgqp,pkd->rqkgd", shared_gscore, shared_keys, preferred_element_type=jnp.float32
    ) + jnp.einsum("rkgqj,rjkd->rqkgd", own_gscore, own_keys, preferred_element_type=jnp.float32)
    return query_gradient.astype(jnp.bfloat16)


def attend_rows(
    query_rows,
    key_own,
    value_own,
    base_rows,
    row_loss_weight,
    row_len,
    prompt_index,
    cache_keys,
    cache_values,
    key_prompt,
    key_place,
    head_groups,
):
    row_count = query_rows.shape[0]
    kv_local = cache_keys.shape[1] // HEAD_WIDTH
    shared_keys = cache_keys.reshape(cache_keys.shape[0], kv_local, HEAD_WIDTH)
    shared_values = cache_values.reshape(cache_values.shape[0], kv_local, HEAD_WIDTH)
    block_of_rows = math.gcd(row_count, 16)

    def one_block(block_index):
        first_row = block_index * block_of_rows

        def rows_of(array):
            return lax.dynamic_slice_in_dim(array, first_row, block_of_rows, 0)

        head_shape = (block_of_rows, QUERY_LENGTH, kv_local, head_groups, HEAD_WIDTH)
        own_shape = (block_of_rows, QUERY_LENGTH, kv_local, HEAD_WIDTH)
        grad_rows = attend_block(
            rows_of(query_rows).reshape(head_shape),
            rows_of(key_own).reshape(own_shape),
            rows_of(value_own).reshape(own_shape),
            rows_of(base_rows).reshape(head_shape),
            rows_of(row_loss_weight),
            rows_of(row_len),
            rows_of(prompt_index),
            shared_keys,
            shared_values,
            key_prompt,
            key_place,
        )
        return grad_rows.reshape(block_of_rows, -1)

    grad_rows = lax.map(one_block, jnp.arange(row_count // block_of_rows, dtype=jnp.int32))
    return grad_rows.reshape(row_count, -1)


def apply_rank_update(flat_tokens, token_onehot, down_weight_flat, up_weight_flat):
    token_count = flat_tokens.shape[0]
    adapters = token_onehot.shape[1]
    all_ranks = lax.dot_general(
        flat_tokens, down_weight_flat, (((1,), (1,)), ((), ())), preferred_element_type=jnp.float32
    )
    value_partial = jnp.sum(
        all_ranks.reshape(token_count, adapters, -1) * token_onehot[:, :, None], axis=1
    )
    rank_projection = lax.psum(value_partial, "kv").astype(jnp.bfloat16)
    rank_spread = (
        token_onehot.astype(jnp.bfloat16)[:, :, None] * rank_projection[:, None, :]
    ).reshape(token_count, -1)
    adapter_delta = (
        ADAPTER_SCALE * jnp.dot(rank_spread, up_weight_flat, preferred_element_type=jnp.float32)
    ).astype(jnp.bfloat16)
    return (rank_spread, adapter_delta)


def low_rank_grads(flat_tokens, token_onehot, rank_spread, query_gradient, up_weight_flat):
    token_count = flat_tokens.shape[0]
    adapters = token_onehot.shape[1]
    up_gradient = ADAPTER_SCALE * lax.dot_general(
        rank_spread, query_gradient, (((0,), (0,)), ((), ())), preferred_element_type=jnp.float32
    )
    all_ranks = lax.dot_general(
        query_gradient, up_weight_flat, (((1,), (1,)), ((), ())), preferred_element_type=jnp.float32
    )
    value_partial = jnp.sum(
        all_ranks.reshape(token_count, adapters, -1) * token_onehot[:, :, None], axis=1
    )
    rank_gradient = (
        ADAPTER_SCALE * lax.psum(value_partial.astype(jnp.bfloat16), "kv").astype(jnp.float32)
    ).astype(jnp.bfloat16)
    grad_spread = (
        token_onehot.astype(jnp.bfloat16)[:, :, None] * rank_gradient[:, None, :]
    ).reshape(token_count, -1)
    down_grad = lax.dot_general(
        grad_spread, flat_tokens, (((0,), (0,)), ((), ())), preferred_element_type=jnp.float32
    )
    return (down_grad, up_gradient)


def per_device(
    tokens,
    frozen_query,
    trained_keys,
    trained_values,
    frozen_output,
    prompt_key_cache,
    prompt_value_cache,
    adapter_down,
    adapter_up,
    row_adapter_index,
    row_forget_flag,
    row_prompt_index,
    row_prompt_length,
):
    tok_count = lax.axis_size("tok")
    my_index = lax.axis_index("tok")
    rows_dev = tokens.shape[0] // QUERY_LENGTH
    adapter_local = adapter_down.shape[0]
    capacity = max(2, 2 * rows_dev // tok_count)
    adapter_slot_count = tok_count * capacity
    head_groups = QUERY_HEADS // KEY_HEADS
    down_weight_flat = adapter_down.reshape(adapter_local * ADAPTER_RANK, -1)
    up_weight_flat = adapter_up.reshape(adapter_local * ADAPTER_RANK, -1)
    prompt_count = prompt_key_cache.shape[0]
    place_local = prompt_key_cache.shape[1]
    flat_key_cache = prompt_key_cache.reshape(prompt_count * place_local, -1)
    flat_value_cache = prompt_value_cache.reshape(prompt_count * place_local, -1)
    cache_keys, cache_values = (
        lax.all_to_all(flat_key_cache, "kv", split_axis=1, concat_axis=0, tiled=True),
        lax.all_to_all(flat_value_cache, "kv", split_axis=1, concat_axis=0, tiled=True),
    )
    key_slots = jnp.arange(cache_keys.shape[0], dtype=jnp.int32)
    key_prompt = key_slots // place_local % prompt_count
    key_place = key_slots // (prompt_count * place_local) * place_local + key_slots % place_local
    owners_all = (row_adapter_index // adapter_local).reshape(tok_count, rows_dev)
    ranks_all = slot_ranks(owners_all)
    my_owners = lax.dynamic_index_in_dim(owners_all, my_index, 0, keepdims=False)
    my_ranks = lax.dynamic_index_in_dim(ranks_all, my_index, 0, keepdims=False)
    target = my_owners * capacity + my_ranks
    selector = (jnp.arange(adapter_slot_count, dtype=jnp.int32)[:, None] == target[None, :]).astype(
        jnp.bfloat16
    )
    matched = (owners_all == my_index)[:, None, :] & (
        ranks_all[:, None, :] == jnp.arange(capacity, dtype=jnp.int32)[None, :, None]
    )
    present = jnp.any(matched, axis=2).reshape(adapter_slot_count)
    local_row = jnp.sum(matched.astype(jnp.int32) * jnp.arange(rows_dev, dtype=jnp.int32), axis=2)
    slot_rows = (jnp.arange(tok_count, dtype=jnp.int32)[:, None] * rows_dev + local_row).reshape(
        adapter_slot_count
    )
    slot_adapter = row_adapter_index[slot_rows] % adapter_local
    slot_hot = (
        (slot_adapter[:, None] == jnp.arange(adapter_local, dtype=jnp.int32)[None, :])
        & present[:, None]
    ).astype(jnp.float32)
    token_onehot = jnp.repeat(slot_hot, QUERY_LENGTH, axis=0)
    shifted_values = (
        lax.all_to_all(
            route_rows(selector, tokens), "tok", split_axis=0, concat_axis=0, tiled=True
        ),
        lax.all_to_all(
            route_rows(selector, frozen_query), "tok", split_axis=0, concat_axis=0, tiled=True
        ),
        lax.all_to_all(
            route_rows(selector, trained_keys), "tok", split_axis=0, concat_axis=0, tiled=True
        ),
        lax.all_to_all(
            route_rows(selector, trained_values), "tok", split_axis=0, concat_axis=0, tiled=True
        ),
        lax.all_to_all(
            route_rows(selector, frozen_output), "tok", split_axis=0, concat_axis=0, tiled=True
        ),
    )
    flat_tokens = shifted_values[0].reshape(adapter_slot_count * QUERY_LENGTH, -1)
    rank_spread, adapter_delta = apply_rank_update(
        flat_tokens, token_onehot, down_weight_flat, up_weight_flat
    )
    query_rows = (
        shifted_values[1].reshape(adapter_slot_count * QUERY_LENGTH, -1).astype(jnp.float32)
        + adapter_delta.astype(jnp.float32)
    ).astype(jnp.bfloat16)
    slot_weight = jnp.where(
        present, 1.0 - 2.0 * row_forget_flag[slot_rows].astype(jnp.float32), 0.0
    )
    query_gradient = attend_rows(
        query_rows.reshape(adapter_slot_count, -1),
        shifted_values[2],
        shifted_values[3],
        shifted_values[4],
        slot_weight,
        row_prompt_length[slot_rows],
        row_prompt_index[slot_rows],
        cache_keys,
        cache_values,
        key_prompt,
        key_place,
        head_groups,
    )
    query_gradient = query_gradient.reshape(adapter_slot_count * QUERY_LENGTH, -1)
    down_grad, up_gradient = low_rank_grads(
        flat_tokens, token_onehot, rank_spread, query_gradient, up_weight_flat
    )
    return (
        down_grad.reshape(adapter_local, ADAPTER_RANK, -1).astype(jnp.bfloat16),
        up_gradient.reshape(adapter_local, ADAPTER_RANK, -1).astype(jnp.bfloat16),
    )


def solution(mesh):
    return jax.shard_map(
        per_device,
        mesh=mesh,
        in_specs=(
            P("tok", "kv"),
            P("tok", "kv"),
            P("tok", "kv"),
            P("tok", "kv"),
            P("tok", "kv"),
            P(None, "kv", None),
            P(None, "kv", None),
            P("tok", None, "kv"),
            P("tok", None, "kv"),
            P(),
            P(),
            P(),
            P(),
        ),
        out_specs=(P("tok", None, "kv"), P("tok", None, "kv")),
        check_vma=False,
    )
```

profile of v0, /device:TPU:9, one launch (start us, length us, event | category | flops | bytes accessed | tf_op | source)
XLA Modules:
  0.0 855.8 jit_solution(9205593096798144714)
XLA Ops:
  9.2 4.0 all-to-all-start.2
  23.6 4.1 all-to-all-done.4
  27.6 15.0 %all-to-all-start.3 = ((bf16[64,2,2048]{2,1,0:T(2,128)(2,1)}), bf16[64,2,2048]{2,1,0:T(2,128)(2,1)S(1)}, u32[]{:S(2)}, u32[]{:S(2)}) async-start(bf16[64,2,2048]{2,1,0:T(2,128)(2,1)} %all_to_all.67), calls=%async_computation.3 | async-start | bytes 1048576 | tf_op jit(solution)/shard_map/all_to_all | solution.py:258
  44.1 15.9 %all-to-all-done.3 = bf16[64,2,2048]{2,1,0:T(2,128)(2,1)S(1)} async-done(((bf16[64,2,2048]{2,1,0:T(2,128)(2,1)}), bf16[64,2,2048]{2,1,0:T(2,128)(2,1)S(1)}, u32[]{:S(2)}, u32[]{:S(2)}) %all-to-all-start.3) | async-done | bytes 524320 | tf_op jit(solution)/shard_map/all_to_all | solution.py:258
  60.1 6.0 all-to-all-start.5
  70.8 7.7 all_to_all.62
  78.5 5.0 all-to-all-done.5
  83.5 6.2 all-to-all-start.1
  94.4 7.7 all_to_all.60
  102.1 81.5 %all-to-all-done.1 = bf16[64,2,16384]{2,1,0:T(2,128)(2,1)} async-done(((bf16[64,2,16384]{2,1,0:T(2,128)(2,1)}), bf16[64,2,16384]{2,1,0:T(2,128)(2,1)}, u32[]{:S(2)}, u32[]{:S(2)}) %all-to-all-start.1) | async-done | bytes 4194336 | tf_op jit(solution)/shard_map/all_to_all | solution.py:252
  183.6 7.9 all-to-all-start
  196.3 7.6 all_to_all.76
  203.9 81.5 %all-to-all-done = bf16[64,2,16384]{2,1,0:T(2,128)(2,1)} async-done(((bf16[64,2,16384]{2,1,0:T(2,128)(2,1)}), bf16[64,2,16384]{2,1,0:T(2,128)(2,1)}, u32[]{:S(2)}, u32[]{:S(2)}) %all-to-all-start) | async-done | bytes 4194336 | tf_op jit(solution)/shard_map/all_to_all | solution.py:255
  285.4 8.5 all-to-all-start.6
  303.1 7.8 reshape.320
  311.0 3.8 fusion.66
  314.8 8.0 reshape.277
  322.8 15.3 %all-reduce.4 = bf16[1024,64]{0,1:T(8,128)(2,1)S(1)} all-reduce(f32[1024,64]{0,1:T(8,128)S(1)} %fusion.66), channel_id=1, replica_groups=mesh['tok'=64,'kv'=4] {'kv'}, use_global_device_ids=true, to_apply=%region_4.5 | all-reduce | flops 65536 | bytes 393216 | tf_op jit(solution)/shard_map/psum | solution.py:160
  338.1 6.6 add_convert_fusion
  344.7 7.4 reshape.270
  353.0 34.7 %all-to-all-done.6 = bf16[64,2,16384]{2,1,0:T(2,128)(2,1)} async-done(((bf16[64,2,16384]{2,1,0:T(2,128)(2,1)}), bf16[64,2,16384]{2,1,0:T(2,128)(2,1)}, u32[]{:S(2)}, u32[]{:S(2)}) %all-to-all-start.6) | async-done | bytes 4194336 | tf_op jit(solution)/shard_map/all_to_all | solution.py:264
  387.7 7.2 all_to_all.78
  394.9 388.6 %while.11 = (s32[]{:T(128)}, bf16[8,16,16384]{2,1,0:T(8,128)(2,1)}, s32[8]{0:T(128)S(1)}, s32[128]{0:T(128)S(1)}, s32[128]{0:T(128)S(1)}, /*index=5*/bf16[128,16...) while((s32[]{:T(128)}, bf16[8,16,16384]{2,1,0:T(8,128)(2,1)}, ...), condition=%wide.region_12.13_spmd.clone, body=%wide.region_5.12_spmd.clone.sunk | while | flops 1124337152 | bytes 62347452 | solution.py:147
  429.6 4.8 fusion.147
  435.9 4.4 fusion.150
  478.2 4.8 fusion.147
  484.5 4.4 fusion.150
  505.5 3.6 fusion.141
  526.7 4.8 fusion.147
  533.0 4.4 fusion.150
  554.0 3.6 fusion.141
  575.2 4.8 fusion.147
  581.5 4.4 fusion.150
  602.5 3.6 fusion.141
  623.7 4.8 fusion.147
  630.0 4.4 fusion.150
  672.3 4.8 fusion.147
  678.6 4.4 fusion.150
  720.8 4.8 fusion.147
  727.1 4.4 fusion.150
  769.3 4.8 fusion.147
  775.6 4.4 fusion.150
  783.5 7.4 reshape_reshape.3
  790.9 7.4 reshape.322
  798.3 4.2 fusion.67
  802.6 4.4 fusion.65
  807.0 36.3 %all-reduce.3.cloned.1.call-done = bf16[1024,64]{0,1:T(8,128)(2,1)} async-done(((bf16[1024,64]{0,1:T(8,128)(2,1)}), bf16[1024,64]{0,1:T(8,128)(2,1)}) %all-reduce.3.cloned.1.call-update) | async-done | bytes 131088 | tf_op jit(solution)/shard_map/psum | solution.py:183
  844.3 4.4 convolution_convert_fusion.3
  (585 shorter events, 335.3 us)
Async XLA Ops:
  7.2 330.9 %copy-start = (bf16[4,64,2048]{2,1,0:T(8,128)(2,1)S(1)}, bf16[4,64,2048]{2,1,0:T(8,128)(2,1)}, u32[]{:S(2)}) copy-start(bf16[4,64,2048]{2,1,0:T(8,128)(2,1)} %param.23) | copy-start | bytes 3145732
  7.2 35.4 %copy-start.14 = (bf16[256,256]{1,0:T(8,128)(2,1)S(1)}, bf16[256,256]{1,0:T(8,128)(2,1)}, u32[]{:S(2)}) copy-start(bf16[256,256]{1,0:T(8,128)(2,1)} %param.18) | copy-start | bytes 393220
  9.2 9.6 %all-to-all-start.2 = ((bf16[128,4,256]{2,0,1:T(8,128)(2,1)}), bf16[128,4,256]{2,0,1:T(8,128)(2,1)S(1)}, u32[]{:S(2)}, u32[]{:S(2)}) async-start(bf16[128,4,256]{2,0,1:T(8,128)(2,1)} %copy.196), calls=%async_computation.2 | async-start | bytes 524288 | tf_op jit(solution)/shard_map/all_to_all | solution.py:223
  18.7 8.9 %all-to-all-start.4 = ((bf16[128,4,256]{2,0,1:T(8,128)(2,1)}), bf16[128,4,256]{2,0,1:T(8,128)(2,1)S(1)}, u32[]{:S(2)}, u32[]{:S(2)}) async-start(bf16[128,4,256]{2,0,1:T(8,128)(2,1)} %copy.197), calls=%async_computation.4 | async-start | bytes 524288 | tf_op jit(solution)/shard_map/all_to_all | solution.py:224
  27.6 32.4 %copy-start.11 = (bf16[128,4,256]{2,0,1:T(8,128)(2,1)}, bf16[128,4,256]{2,0,1:T(8,128)(2,1)S(1)}, u32[]{:S(2)}) copy-start(bf16[128,4,256]{2,0,1:T(8,128)(2,1)S(1)} %all-to-all-done.4) | copy-start | bytes 786436
  27.6 32.4 %all-to-all-start.3 = ((bf16[64,2,2048]{2,1,0:T(2,128)(2,1)}), bf16[64,2,2048]{2,1,0:T(2,128)(2,1)S(1)}, u32[]{:S(2)}, u32[]{:S(2)}) async-start(bf16[64,2,2048]{2,1,0:T(2,128)(2,1)} %all_to_all.67), calls=%async_computation.3 | async-start | bytes 1048576 | tf_op jit(solution)/shard_map/all_to_all | solution.py:258
  60.1 23.4 %all-to-all-start.5 = ((bf16[64,2,2048]{2,1,0:T(2,128)(2,1)}), bf16[64,2,2048]{2,1,0:T(2,128)(2,1)S(1)}, u32[]{:S(2)}, u32[]{:S(2)}) async-start(bf16[64,2,2048]{2,1,0:T(2,128)(2,1)} %all_to_all.73), calls=%async_computation.5 | async-start | bytes 1048576 | tf_op jit(solution)/shard_map/all_to_all | solution.py:261
  83.5 100.1 %all-to-all-start.1 = ((bf16[64,2,16384]{2,1,0:T(2,128)(2,1)}), bf16[64,2,16384]{2,1,0:T(2,128)(2,1)}, u32[]{:S(2)}, u32[]{:S(2)}) async-start(bf16[64,2,16384]{2,1,0:T(2,128)(2,1)} %all_to_all.62), calls=%async_computation.1 | async-start | bytes 8388608 | tf_op jit(solution)/shard_map/all_to_all | solution.py:252
  183.6 101.7 %all-to-all-start = ((bf16[64,2,16384]{2,1,0:T(2,128)(2,1)}), bf16[64,2,16384]{2,1,0:T(2,128)(2,1)}, u32[]{:S(2)}, u32[]{:S(2)}) async-start(bf16[64,2,16384]{2,1,0:T(2,128)(2,1)} %all_to_all.60), calls=%async_computation | async-start | bytes 8388608 | tf_op jit(solution)/shard_map/all_to_all | solution.py:255
  203.9 90.5 %copy-start.1 = (s32[2048]{0:T(1024)S(1)}, s32[2048]{0:T(1024)}, u32[]{:S(2)}) copy-start(s32[2048]{0:T(1024)} %param.24) | copy-start | bytes 24580
  203.9 92.3 %copy-start.2 = (s32[2048]{0:T(1024)S(1)}, s32[2048]{0:T(1024)}, u32[]{:S(2)}) copy-start(s32[2048]{0:T(1024)} %param.25) | copy-start | bytes 24580
  203.9 93.5 %copy-start.3 = (s32[2048]{0:T(1024)S(1)}, s32[2048]{0:T(1024)}, u32[]{:S(2)}) copy-start(s32[2048]{0:T(1024)} %param.26) | copy-start | bytes 24580
  203.9 94.6 %copy-start.4 = (s32[2048]{0:T(1024)S(1)}, s32[2048]{0:T(1024)}, u32[]{:S(2)}) copy-start(s32[2048]{0:T(1024)} %param.27) | copy-start | bytes 24580
  203.9 96.4 %copy-start.12 = (bf16[128,4,256]{2,0,1:T(8,128)(2,1)S(1)}, bf16[128,4,256]{2,0,1:T(8,128)(2,1)}, u32[]{:S(2)}) copy-start(bf16[128,4,256]{2,0,1:T(8,128)(2,1)} %copy-done.11) | copy-start | bytes 786436
  285.4 102.4 %all-to-all-start.6 = ((bf16[64,2,16384]{2,1,0:T(2,128)(2,1)}), bf16[64,2,16384]{2,1,0:T(2,128)(2,1)}, u32[]{:S(2)}, u32[]{:S(2)}) async-start(bf16[64,2,16384]{2,1,0:T(2,128)(2,1)} %all_to_all.76), calls=%async_computation.6 | async-start | bytes 8388608 | tf_op jit(solution)/shard_map/all_to_all | solution.py:264
  293.9 549.5 %all-reduce.3.cloned.1.call-start = ((), (), s32[]{:S(2)}) async-start(), calls=%async_computation.7 | async-start | bytes 262144 | tf_op jit(solution)/shard_map/psum | solution.py:183
  296.1 14.9 %copy-start.15 = (f32[1024,4]{0,1:T(4,128)}, f32[1024,4]{0,1:T(4,128)S(1)}, u32[]{:S(2)}) copy-start(f32[1024,4]{0,1:T(4,128)S(1)} %reshape.266) | copy-start | bytes 49156
  296.2 55.9 %copy-start.17 = (bf16[1024,4]{0,1:T(4,128)(2,1)}, bf16[1024,4]{0,1:T(4,128)(2,1)S(1)}, u32[]{:S(2)}) copy-start(bf16[1024,4]{0,1:T(4,128)(2,1)S(1)} %convert_element_type.96) | copy-start | bytes 24580
  395.1 5.6 copy-start.5
  395.1 5.6 copy-start.19
  395.1 5.6 copy-start.21
  435.9 6.2 copy-start.8
  443.6 5.6 copy-start.5
  443.6 5.6 copy-start.19
  443.7 5.6 copy-start.21
  484.5 6.2 copy-start.8
  492.2 5.6 copy-start.5
  492.2 5.6 copy-start.19
  533.0 6.2 copy-start.8
  540.7 5.6 copy-start.5
  540.7 5.6 copy-start.19
  581.5 6.2 copy-start.8
  589.2 5.6 copy-start.5
  589.2 5.6 copy-start.19
  630.0 6.2 copy-start.8
  637.7 5.6 copy-start.5
  637.7 5.6 copy-start.19
  637.7 5.6 copy-start.21
  678.6 6.2 copy-start.8
  686.3 5.6 copy-start.5
  686.3 5.6 copy-start.19
  727.1 6.2 copy-start.8
  734.8 5.6 copy-start.5
  734.8 5.6 copy-start.19
  734.8 5.6 copy-start.21
  775.6 6.2 copy-start.8
  790.9 7.4 copy-start.16
  802.6 41.7 %copy-start.18 = (bf16[1024,4]{0,1:T(4,128)(2,1)S(1)}, bf16[1024,4]{0,1:T(4,128)(2,1)}, u32[]{:S(2)}) copy-start(bf16[1024,4]{0,1:T(4,128)(2,1)} %copy-done.17) | copy-start | bytes 24580
  (53 other events, 193.4 us)
Sparse Core Ops, SparseCore 0:
  802.7 40.5 all-reduce.2
where the time goes:
time: 871 us; the launch traced here: 856 us
  waiting for transfers between devices  260 us (30%)
  local copies, waits for them, and re-layouts  194 us (22%)
  matrix products  192 us (22%)
  other arithmetic  121 us (14%)
  starting transfers between devices  51 us (6%)
  blocking collectives  15.3 us (2%)
  between operations  14.7 us (2%)
    all_to_all x1, waiting for transfers between devices, per_device(): lax.all_to_all(route_rows(selector, tokens), 'tok', split_axis=0, concat_...  81.5 us
    all_to_all x1, waiting for transfers between devices, per_device(): lax.all_to_all(route_rows(selector, frozen_query), 'tok', split_axis=0, c...  81.5 us
    dot_general x8, matrix products, attend_block(): jnp.einsum('rqkgd,pkd->rkgqp', grad_out, shared_values, preferred_element...  38.4 us
    psum x1, waiting for transfers between devices, low_rank_grads(): lax.psum(value_partial.astype(jnp.bfloat16), 'kv').astype(jnp.float32)  36.3 us
    convert_element_type x8, other arithmetic, attend_block(): (shared_probs * (shared_grad - inner_sum) * inv_root).astype(jnp.bfloat16)  35.3 us
    all_to_all x1, waiting for transfers between devices, per_device(): lax.all_to_all(route_rows(selector, frozen_output), 'tok', split_axis=0,...  34.7 us
    reduce_sum x8, other arithmetic, attend_block(): jnp.sum(shared_exp, axis=-1, keepdims=True)  28.8 us
    dot_general x8, matrix products, attend_block(): jnp.einsum('rqkgd,rjkd->rkgqj', query_rows, own_keys, preferred_element_t...  27.1 us
  transfers between devices with their start and end apart: 8, of which 8 were waited for; matrix products, arithmetic and copies ran while one was open for 7% of the time, Pallas kernels for 0%

commit v1 on v0

v1 whole, which is shorter than its diff:
```python
import functools
import math

import jax
import jax.numpy as jnp
from jax import lax
from jax.experimental import pallas as pl
from jax.experimental.pallas import tpu as pltpu
from jax.sharding import PartitionSpec as P

QUERY_HEADS = 64
KEY_HEADS = 8
HEAD_WIDTH = 128
ADAPTER_RANK = 64
QUERY_LENGTH = 8
ADAPTER_SCALE = 0.5
CAP = 2
ROW_BLOCK = 16
VMEM_LIMIT = 56 * 1024 * 1024

_VMEM = pl.BlockSpec(memory_space=pltpu.VMEM)
_SMEM = pl.BlockSpec(memory_space=pltpu.SMEM)
_ANY = pl.BlockSpec(memory_space=pl.ANY)


def params():
    return pltpu.CompilerParams(vmem_limit_bytes=VMEM_LIMIT)


def route_kernel(source_ref, rows_ref, out_ref):
    first = pl.program_id(0) * out_ref.shape[0]
    for j in range(out_ref.shape[0]):
        row = source_ref[first + j]

        @pl.when(row >= 0)
        def _():
            out_ref[j] = rows_ref[row]

        @pl.when(row < 0)
        def _():
            out_ref[j] = jnp.zeros_like(out_ref[j])


def route_rows(source, rows, slots):
    row_count, length, width = rows.shape
    step = 16
    return pl.pallas_call(
        route_kernel,
        grid_spec=pltpu.PrefetchScalarGridSpec(
            num_scalar_prefetch=1,
            grid=(slots // step,),
            in_specs=[pl.BlockSpec((row_count, length, width), lambda i, s: (0, 0, 0))],
            out_specs=pl.BlockSpec((step, length, width), lambda i, s: (i, 0, 0)),
        ),
        out_shape=jax.ShapeDtypeStruct((slots, length, width), rows.dtype),
        compiler_params=params(),
        name="route_rows",
    )(source, rows)


def fold(products, mask):
    kept = products * mask.astype(jnp.float32)
    half = kept[:, :128] + kept[:, 128:]
    return half + pltpu.roll(half, 64, 1)


def low_half(shape):
    return lax.broadcasted_iota(jnp.int32, shape, 1) < 64


def project_kernel(xa_ref, xb_ref, ma_ref, mb_ref, weight_ref, out_ref):
    dims = (((1,), (1,)), ((), ()))
    weight = weight_ref[...]
    first = lax.dot_general(xa_ref[...], weight, dims, preferred_element_type=jnp.float32)
    second = lax.dot_general(xb_ref[...], weight, dims, preferred_element_type=jnp.float32)
    both = jnp.where(
        low_half(out_ref.shape), fold(first, ma_ref[...]), fold(second, mb_ref[...])
    )
    out_ref[...] = both.astype(out_ref.dtype)


def project(x, mask, weight, out_type):
    tokens, width = x.shape
    ranks = weight.shape[0]
    half = tokens // 2
    block = 128
    steps = half // block
    return pl.pallas_call(
        project_kernel,
        grid=(steps,),
        in_specs=[
            pl.BlockSpec((block, width), lambda i: (i, 0)),
            pl.BlockSpec((block, width), lambda i: (i + steps, 0)),
            pl.BlockSpec((block, ranks), lambda i: (i, 0)),
            pl.BlockSpec((block, ranks), lambda i: (i + steps, 0)),
            pl.BlockSpec((ranks, width), lambda i: (0, 0)),
        ],
        out_specs=pl.BlockSpec((block, 128), lambda i: (i, 0)),
        out_shape=jax.ShapeDtypeStruct((half, 128), out_type),
        compiler_params=params(),
        name="project",
    )(x, x, mask, mask, weight)


def spread_of(packed, mask, is_low):
    low = low_half(packed.shape)
    turned = pltpu.roll(packed, 64, 1)
    twice = jnp.where(low, packed, turned) if is_low else jnp.where(low, turned, packed)
    return (jnp.concatenate([twice, twice], axis=1) * mask.astype(jnp.float32)).astype(
        jnp.bfloat16
    )


def delta_kernel(p0, p1, p2, p3, mask_ref, weight_ref, out_ref, spread_ref, *, steps):
    total = (p0[...] + p1[...]) + (p2[...] + p3[...])
    low_rank = total.astype(jnp.bfloat16).astype(jnp.float32)

    def finish(is_low):
        spread = spread_of(low_rank, mask_ref[...], is_low)
        spread_ref[...] = spread
        out_ref[...] = (
            ADAPTER_SCALE
            * jnp.dot(spread, weight_ref[...], preferred_element_type=jnp.float32)
        ).astype(out_ref.dtype)

    pl.when(pl.program_id(0) < steps)(lambda: finish(True))
    pl.when(pl.program_id(0) >= steps)(lambda: finish(False))


def make_delta(parts, mask, weight):
    half = parts[0].shape[0]
    ranks, width = weight.shape
    block = 128
    steps = half // block
    packed = pl.BlockSpec((block, 128), lambda i: (i % steps, 0))
    return pl.pallas_call(
        functools.partial(delta_kernel, steps=steps),
        grid=(2 * steps,),
        in_specs=[packed] * 4
        + [
            pl.BlockSpec((block, ranks), lambda i: (i, 0)),
            pl.BlockSpec((ranks, width), lambda i: (0, 0)),
        ],
        out_specs=[
            pl.BlockSpec((block, width), lambda i: (i, 0)),
            pl.BlockSpec((block, ranks), lambda i: (i, 0)),
        ],
        out_shape=[
            jax.ShapeDtypeStruct((2 * half, width), jnp.bfloat16),
            jax.ShapeDtypeStruct((2 * half, ranks), jnp.bfloat16),
        ],
        compiler_params=params(),
        name="make_delta",
    )(*parts, mask, weight)


def grad_up_kernel(spread_ref, gradient_ref, out_ref):
    out_ref[...] = (
        ADAPTER_SCALE
        * lax.dot_general(
            spread_ref[...],
            gradient_ref[...],
            (((0,), (0,)), ((), ())),
            preferred_element_type=jnp.float32,
        )
    ).astype(out_ref.dtype)


def grad_up(spread, gradient):
    tokens, ranks = spread.shape
    width = gradient.shape[1]
    block = 512
    return pl.pallas_call(
        grad_up_kernel,
        grid=(width // block,),
        in_specs=[
            pl.BlockSpec((tokens, ranks), lambda i: (0, 0)),
            pl.BlockSpec((tokens, block), lambda i: (0, i)),
        ],
        out_specs=pl.BlockSpec((ranks, block), lambda i: (0, i)),
        out_shape=jax.ShapeDtypeStruct((ranks, width), jnp.bfloat16),
        compiler_params=params(),
        name="grad_up",
    )(spread, gradient)


def grad_down_kernel(p0, p1, p2, p3, mask_ref, tokens_ref, out_ref, spread_ref):
    half = p0.shape[0]

    @pl.when(pl.program_id(0) == 0)
    def _():
        total = (p0[...].astype(jnp.float32) + p1[...].astype(jnp.float32)) + (
            p2[...].astype(jnp.float32) + p3[...].astype(jnp.float32)
        )
        low_grad = (ADAPTER_SCALE * total).astype(jnp.bfloat16).astype(jnp.float32)
        spread_ref[:half] = spread_of(low_grad, mask_ref[:half], True)
        spread_ref[half:] = spread_of(low_grad, mask_ref[half:], False)

    out_ref[...] = lax.dot_general(
        spread_ref[...],
        tokens_ref[...],
        (((0,), (0,)), ((), ())),
        preferred_element_type=jnp.float32,
    ).astype(out_ref.dtype)


def grad_down(parts, mask, x):
    half = parts[0].shape[0]
    ranks = mask.shape[1]
    tokens, width = x.shape
    block = 512
    return pl.pallas_call(
        grad_down_kernel,
        grid=(width // block,),
        in_specs=[pl.BlockSpec((half, 128), lambda i: (0, 0))] * 4
        + [
            pl.BlockSpec((tokens, ranks), lambda i: (0, 0)),
            pl.BlockSpec((tokens, block), lambda i: (0, i)),
        ],
        out_specs=pl.BlockSpec((ranks, block), lambda i: (0, i)),
        out_shape=jax.ShapeDtypeStruct((ranks, width), jnp.bfloat16),
        scratch_shapes=[pltpu.VMEM((tokens, ranks), jnp.bfloat16)],
        compiler_params=params(),
        name="grad_down",
    )(*parts, mask, x)


def attend_kernel(
    target_ref,
    query_ref,
    base_ref,
    own_key_ref,
    own_value_ref,
    key_ref,
    value_ref,
    row_len_ref,
    row_prompt_ref,
    row_weight_ref,
    key_prompt_ref,
    key_place_ref,
    delta_hbm,
    out_hbm,
    delta_ref,
    grad_ref,
    in_sem,
    out_sem,
):
    rows, length, width = query_ref.shape
    head_group = QUERY_HEADS // KEY_HEADS
    kv_local = key_ref.shape[1] // HEAD_WIDTH
    group_width = head_group * HEAD_WIDTH
    block_tokens = ROW_BLOCK * length
    inv_root = 1.0 / math.sqrt(HEAD_WIDTH)
    queries = head_group * block_tokens
    contract = (((1,), (1,)), ((), ()))

    def fetch(r):
        return pltpu.make_async_copy(delta_hbm.at[target_ref[r]], delta_ref.at[r], in_sem.at[r])

    def send(r):
        return pltpu.make_async_copy(grad_ref.at[r], out_hbm.at[target_ref[r]], out_sem.at[r])

    for r in range(rows):
        fetch(r).start()
    for r in range(rows):
        fetch(r).wait()

    def heads(x):
        return jnp.concatenate(
            [x[:, h * HEAD_WIDTH : (h + 1) * HEAD_WIDTH] for h in range(head_group)], axis=0
        )

    def one_block(b, carry):
        block = pl.ds(b * ROW_BLOCK, ROW_BLOCK)
        tokens = pl.ds(b * block_tokens, block_tokens)
        shared_seen = (row_prompt_ref[tokens, :] == key_prompt_ref[...]) & (
            key_place_ref[...] < row_len_ref[tokens, :]
        )
        own_shape = (block_tokens, block_tokens)
        q_at = lax.broadcasted_iota(jnp.int32, own_shape, 0)
        k_at = lax.broadcasted_iota(jnp.int32, own_shape, 1)
        own_seen = (q_at // length == k_at // length) & (k_at <= q_at)
        weight = row_weight_ref[tokens, :]

        def group(x):
            return x.reshape(head_group, block_tokens, x.shape[-1])

        def flat(x):
            return x.reshape(queries, x.shape[-1])

        for g in range(kv_local):
            columns = slice(g * group_width, (g + 1) * group_width)
            keys_at = slice(g * HEAD_WIDTH, (g + 1) * HEAD_WIDTH)
            query = query_ref[block, :, columns].astype(jnp.float32) + delta_ref[
                block, :, columns
            ].astype(jnp.float32)
            query = heads(query.reshape(block_tokens, group_width)).astype(jnp.bfloat16)
            base = heads(
                base_ref[block, :, columns].astype(jnp.float32).reshape(block_tokens, group_width)
            )
            keys = key_ref[:, keys_at]
            values = value_ref[:, keys_at]
            own_keys = (
                own_key_ref[block, :, keys_at]
                .astype(jnp.float32)
                .reshape(block_tokens, HEAD_WIDTH)
                .astype(jnp.bfloat16)
            )
            own_values = (
                own_value_ref[block, :, keys_at]
                .astype(jnp.float32)
                .reshape(block_tokens, HEAD_WIDTH)
                .astype(jnp.bfloat16)
            )

            def by_rows(a, b):
                return lax.dot_general(a, b, contract, preferred_element_type=jnp.float32)

            def times(a, b):
                return jnp.dot(a, b, preferred_element_type=jnp.float32)

            shared = jnp.where(shared_seen[None], group(by_rows(query, keys) * inv_root), -1e30)
            own = jnp.where(own_seen[None], group(by_rows(query, own_keys) * inv_root), -1e30)
            top = jnp.maximum(
                jnp.max(shared, axis=-1, keepdims=True), jnp.max(own, axis=-1, keepdims=True)
            )
            shared = jnp.exp(shared - top)
            own = jnp.exp(own - top)
            total = jnp.sum(shared, axis=-1, keepdims=True) + jnp.sum(own, axis=-1, keepdims=True)
            scale = 1.0 / total
            shared = flat(shared * scale)
            own = flat(own * scale)
            attn_out = times(shared.astype(jnp.bfloat16), values) + times(
                own.astype(jnp.bfloat16), own_values
            )
            grad_out = flat(group(attn_out - base) * weight[None]).astype(jnp.bfloat16)
            shared_grad = by_rows(grad_out, values)
            own_grad = by_rows(grad_out, own_values)
            inner = jnp.sum(shared * shared_grad, axis=-1, keepdims=True) + jnp.sum(
                own * own_grad, axis=-1, keepdims=True
            )
            shared_gs = (shared * (shared_grad - inner) * inv_root).astype(jnp.bfloat16)
            own_gs = (own * (own_grad - inner) * inv_root).astype(jnp.bfloat16)
            gradient = times(shared_gs, keys) + times(own_gs, own_keys)
            for h in range(head_group):
                piece = gradient[h * block_tokens : (h + 1) * block_tokens]
                at = g * group_width + h * HEAD_WIDTH
                grad_ref[block, :, at : at + HEAD_WIDTH] = piece.reshape(
                    ROW_BLOCK, length, HEAD_WIDTH
                ).astype(jnp.bfloat16)
        return carry

    lax.fori_loop(0, rows // ROW_BLOCK, one_block, 0)
    for r in range(rows):
        send(r).start()
    for r in range(rows):
        send(r).wait()


def attend(target, query, base, own_key, own_value, keys, values, per_token, per_key, delta):
    rows, length, width = query.shape
    row_vectors = [v.reshape(rows * length, 1) for v in per_token]
    key_vectors = [v.reshape(1, -1) for v in per_key]
    return pl.pallas_call(
        attend_kernel,
        in_specs=[_SMEM] + [_VMEM] * 11 + [_ANY],
        out_specs=_ANY,
        out_shape=jax.ShapeDtypeStruct(delta.shape, delta.dtype),
        scratch_shapes=[
            pltpu.VMEM((rows, length, width), jnp.bfloat16),
            pltpu.VMEM((rows, length, width), jnp.bfloat16),
            pltpu.SemaphoreType.DMA((rows,)),
            pltpu.SemaphoreType.DMA((rows,)),
        ],
        input_output_aliases={12: 0},
        compiler_params=params(),
        name="attend",
    )(
        target,
        query,
        base,
        own_key,
        own_value,
        keys,
        values,
        *row_vectors,
        *key_vectors,
        delta,
    )


def shifted(block_for, count):
    return [
        lax.ppermute(block_for(k), "kv", [(i, (i + k) % count) for i in range(count)])
        for k in range(1, count)
    ]


def per_device(
    tokens,
    frozen_query,
    trained_keys,
    trained_values,
    frozen_output,
    prompt_key_cache,
    prompt_value_cache,
    adapter_down,
    adapter_up,
    row_adapter_index,
    row_forget_flag,
    row_prompt_index,
    row_prompt_length,
):
    tok_count = lax.axis_size("tok")
    kv_count = lax.axis_size("kv")
    me = lax.axis_index("tok")
    kv = lax.axis_index("kv")
    rows = tokens.shape[0] // QUERY_LENGTH
    width = tokens.shape[1]
    adapters = adapter_down.shape[0]
    slots = tok_count * CAP
    down_flat = adapter_down.reshape(adapters * ADAPTER_RANK, width)
    up_flat = adapter_up.reshape(adapters * ADAPTER_RANK, width)

    def as_rows(x):
        return x.reshape(rows, QUERY_LENGTH, x.shape[1])

    mine = lax.dynamic_slice_in_dim(row_adapter_index, me * rows, rows) // adapters
    row_at = jnp.arange(rows, dtype=jnp.int32)
    my_rank = jnp.sum(
        ((mine[:, None] == mine[None, :]) & (row_at[:, None] > row_at[None, :])).astype(jnp.int32),
        axis=1,
    )
    target = mine * CAP + my_rank
    slot_at = jnp.arange(slots, dtype=jnp.int32)
    source = (
        jnp.sum(jnp.where(slot_at[:, None] == target[None, :], row_at[None, :] + 1, 0), axis=1) - 1
    )

    sent = route_rows(source, as_rows(tokens), slots)
    arrived = lax.all_to_all(sent, "tok", split_axis=0, concat_axis=0, tiled=True)
    flat_tokens = arrived.reshape(slots * QUERY_LENGTH, width)

    all_owners = (row_adapter_index // adapters).reshape(tok_count, rows)
    hit = all_owners == me
    earlier = (
        jnp.sum(
            jnp.where((row_at[:, None] > row_at[None, :])[None], hit[:, None, :], False).astype(
                jnp.int32
            ),
            axis=2,
        )
    )
    local_adapter = (row_adapter_index % adapters).reshape(tok_count, rows)
    slot_adapter = jnp.sum(
        jnp.where(
            hit[:, None, :]
            & (earlier[:, None, :] == jnp.arange(CAP, dtype=jnp.int32)[None, :, None]),
            local_adapter[:, None, :] + 1,
            0,
        ),
        axis=2,
    ).reshape(slots)
    lane_adapter = jnp.arange(adapters * ADAPTER_RANK, dtype=jnp.int32) // ADAPTER_RANK + 1
    mask = jnp.broadcast_to(
        (slot_adapter[:, None] == lane_adapter[None, :]).astype(jnp.bfloat16)[:, None, :],
        (slots, QUERY_LENGTH, lane_adapter.shape[0]),
    ).reshape(slots * QUERY_LENGTH, lane_adapter.shape[0])

    prompts, place_local = prompt_key_cache.shape[:2]
    head_columns = prompt_key_cache.shape[2] // kv_count
    both = jnp.stack([prompt_key_cache, prompt_value_cache]).reshape(
        2 * prompts * place_local, kv_count, head_columns
    )

    def cache_block(k):
        return lax.dynamic_index_in_dim(both, (kv + k) % kv_count, 1, keepdims=False)

    cache = jnp.stack([cache_block(0)] + shifted(cache_block, kv_count)).reshape(
        kv_count, 2, prompts * place_local, head_columns
    )
    cache_keys = cache[:, 0].reshape(-1, head_columns)
    cache_values = cache[:, 1].reshape(-1, head_columns)
    key_at = jnp.arange(cache_keys.shape[0], dtype=jnp.int32)
    key_from = (kv - key_at // (prompts * place_local) + kv_count) % kv_count
    key_prompt = key_at // place_local % prompts
    key_place = key_from * place_local + key_at % place_local

    def of_my_tokens(x):
        return jnp.repeat(lax.dynamic_slice_in_dim(x, me * rows, rows), QUERY_LENGTH)

    row_weight = 1.0 - 2.0 * of_my_tokens(row_forget_flag).astype(jnp.float32)

    part = project(flat_tokens, mask, down_flat, jnp.float32)
    delta, spread = make_delta([part] + shifted(lambda k: part, kv_count), mask, up_flat)
    delta = lax.all_to_all(
        delta.reshape(slots, QUERY_LENGTH, width), "tok", split_axis=0, concat_axis=0, tiled=True
    )

    gradient = attend(
        target,
        as_rows(frozen_query),
        as_rows(frozen_output),
        as_rows(trained_keys),
        as_rows(trained_values),
        cache_keys,
        cache_values,
        (of_my_tokens(row_prompt_length), of_my_tokens(row_prompt_index), row_weight),
        (key_prompt, key_place),
        delta,
    )
    gradient = lax.all_to_all(gradient, "tok", split_axis=0, concat_axis=0, tiled=True).reshape(
        slots * QUERY_LENGTH, width
    )

    part = project(gradient, mask, up_flat, jnp.bfloat16)
    parts = [part] + shifted(lambda k: part, kv_count)
    up_grad = grad_up(spread, gradient)
    down_grad = grad_down(parts, mask, flat_tokens)
    return (
        down_grad.reshape(adapters, ADAPTER_RANK, width),
        up_grad.reshape(adapters, ADAPTER_RANK, width),
    )


def solution(mesh):
    return jax.shard_map(
        per_device,
        mesh=mesh,
        in_specs=(
            P("tok", "kv"),
            P("tok", "kv"),
            P("tok", "kv"),
            P("tok", "kv"),
            P("tok", "kv"),
            P(None, "kv", None),
            P(None, "kv", None),
            P("tok", None, "kv"),
            P("tok", None, "kv"),
            P(),
            P(),
            P(),
            P(),
        ),
        out_specs=(P("tok", None, "kv"), P("tok", None, "kv")),
        check_vma=False,
    )
```

time: 871 us -> 392 us (0.45); the launches traced: 856 us -> 388 us
  matrix products: 192 us -> 0 us
  local copies, waits for them, and re-layouts: 194 us -> 9.88 us
  other arithmetic: 121 us -> 4.2 us
  blocking collectives: 15.3 us -> 102 us
  waiting for transfers between devices: 260 us -> 182 us
  Pallas kernels: 0 us -> 51.6 us
  between operations: 14.7 us -> 0.91 us
  starting transfers between devices: 51 us -> 37.7 us
    dot_general x74 -> x0, matrix products: 192 us -> none  [the longest x8 38.4 us: attend_block(): jnp.einsum('rqkgd,pkd->rkgqp', grad_out, shared_values, preferred_element...]
    all_to_all x0 -> x1, blocking collectives: none -> 102 us  [per_device(): lax.all_to_all(gradient, 'tok', split_axis=0, concat_axis=0, tiled=True)]
    convert_element_type x35 -> x1, other arithmetic: 70.1 us -> 0.08 us  [per_device(): (slot_adapter[:, None] == lane_adapter[None, :]).astype(jnp.bfloat16)]
    pallas_call x0 -> x7, Pallas kernels: none -> 51.6 us  [the longest x1 14.3 us: attend(): pl.pallas_call(attend_kernel, in_specs=[_SMEM] + [_VMEM] * 11 + [_ANY], o...]
    all_to_all x7 -> x2, waiting for transfers between devices: 224 us -> 173 us  [the longest x1 92 us: per_device(): lax.all_to_all(sent, 'tok', split_axis=0, concat_axis=0, tiled=True)]
    all_to_all x12 -> x0, local copies, waits for them, and re-layouts: 38.3 us -> none  [the longest x2 14.8 us: per_device(): lax.all_to_all(route_rows(selector, frozen_output), 'tok', split_axis=0,...]
    psum x1 -> x0, waiting for transfers between devices: 36.3 us -> none  [low_rank_grads(): lax.psum(value_partial.astype(jnp.bfloat16), 'kv').astype(jnp.float32)]
    reduce_sum x26 -> x4, other arithmetic: 34.7 us -> 0.53 us  [the longest x1 0.23 us: per_device(): jnp.sum(jnp.where((row_at[:, None] > row_at[None, :])[None], hit[:, None,...]
  transfers between devices with their start and end apart: 8 -> 11, of which waited for: 8 -> 5; matrix products, arithmetic and copies ran while one was open for 7% -> 2% of each run, Pallas kernels for 0% -> 1%
where the time goes in v1:
time: 392 us; the launch traced here: 388 us
  waiting for transfers between devices  182 us (46%)
  blocking collectives  102 us (26%)
  Pallas kernels  51.6 us (13%)
  starting transfers between devices  37.7 us (10%)
  local copies, waits for them, and re-layouts  9.88 us (3%)
  other arithmetic  4.2 us (1%)
    all_to_all x1, blocking collectives, per_device(): lax.all_to_all(gradient, 'tok', split_axis=0, concat_axis=0, tiled=True)  102 us
    all_to_all x1, waiting for transfers between devices, per_device(): lax.all_to_all(sent, 'tok', split_axis=0, concat_axis=0, tiled=True)  92 us
    all_to_all x1, waiting for transfers between devices, per_device(): lax.all_to_all(delta.reshape(slots, QUERY_LENGTH, width), 'tok', split_ax...  81.2 us
    pallas_call x1, Pallas kernels, attend(): pl.pallas_call(attend_kernel, in_specs=[_SMEM] + [_VMEM] * 11 + [_ANY], o...  14.3 us
    ppermute x9, starting transfers between devices, shifted(): lax.ppermute(block_for(k), 'kv', [(i, (i + k) % count) for i in range(cou...  13.9 us
    pallas_call x2, Pallas kernels, project(): pl.pallas_call(project_kernel, grid=(steps,), in_specs=[pl.BlockSpec((blo...  12.8 us
    all_to_all x1, starting transfers between devices, per_device(): lax.all_to_all(sent, 'tok', split_axis=0, concat_axis=0, tiled=True)  12.7 us
    all_to_all x1, starting transfers between devices, per_device(): lax.all_to_all(delta.reshape(slots, QUERY_LENGTH, width), 'tok', split_ax...  11.1 us
  transfers between devices with their start and end apart: 11, of which 5 were waited for; matrix products, arithmetic and copies ran while one was open for 2% of the time, Pallas kernels for 1%

profile of v1, /device:TPU:9, one launch (start us, length us, event | category | flops | bytes accessed | tf_op | source)
XLA Modules:
  0.0 388.3 jit_solution(4333803503498865414)
XLA Ops:
  0.6 0.8 and_select_fusion.6
  1.4 0.2 convert_reduce_fusion.1
  1.6 0.8 iota_add_fusion
  2.4 0.1 select_reduce_fusion.1
  2.5 0.5 broadcast_add_fusion.source_ref
  3.0 6.1 %route_rows.1 = bf16[128,8,2048]{2,1,0:T(8,128)(2,1)} custom-call(s32[128]{0:T(128)} %broadcast_add_fusion.source_ref, bf16[32,8,2048]{2,1,0:T(8,128)(2,1)} %bitcast.41), custom_call_target="tpu_custom_call" | custom-call | tf_op jit(solution)/shard_map/route_rows/pallas_call | solution.py:47
  9.1 12.7 %all-to-all-start = ((bf16[128,8,2048]{2,1,0:T(8,128)(2,1)}), bf16[128,8,2048]{2,1,0:T(8,128)(2,1)}, u32[]{:S(2)}, u32[]{:S(2)}) async-start(bf16[128,8,2048]{2,1,0:T(8,128)(2,1)} %route_rows.1), calls=%async_computation | async-start | bytes 8388608 | tf_op jit(solution)/shard_map/all_to_all | solution.py:441
  21.9 0.1 copy.22
  22.2 0.2 convert_reduce_fusion
  22.4 0.1 copy.25
  22.5 0.1 eq.94
  22.8 0.9 broadcast_bitcast_fusion.ma_ref.mb_ref.mask_ref
  23.7 92.0 %all-to-all-done = bf16[128,8,2048]{2,1,0:T(8,128)(2,1)} async-done(((bf16[128,8,2048]{2,1,0:T(8,128)(2,1)}), bf16[128,8,2048]{2,1,0:T(8,128)(2,1)}, u32[]{:S(2)}, u32[]{:S(2)}) %all-to-all-start) | async-done | bytes 4194336 | tf_op jit(solution)/shard_map/all_to_all | solution.py:441
  115.7 6.4 %project.2.p0 = f32[512,128]{1,0:T(8,128)} custom-call(bf16[1024,2048]{1,0:T(8,128)(2,1)} %bitcast.12.xa_ref.xb_ref.tokens_ref, bf16[1024,2048]{1,0:T(8,128)(2,1)} %bitcast.12.xa_ref.xb_ref.tokens_ref, bf16[1024,256]{1,0:T(8,128)(2,1)} %broadcast_bitcast_fusion.ma_ref.mb_ref.mask_ref, bf16[1024,256]{1,0:T(8,128)(2,1)} %broadcast_bitcast_fusion.ma_ref.mb_ref.mask_ref, ...), custom_call_target="tpu_custom_call" | custom-call | tf_op jit(solution)/shard_map/project/pallas_call | solution.py:88
  122.1 1.2 collective-permute-start.3
  123.3 2.5 collective-permute-start.4
  125.8 1.1 collective-permute-start.5
  126.9 1.8 collective-permute-done.3.p1
  128.7 6.3 %collective-permute-done.4.p2 = f32[512,128]{1,0:T(8,128)S(1)} collective-permute-done((f32[512,128]{1,0:T(8,128)}, f32[512,128]{1,0:T(8,128)S(1)}, u32[]{:S(2)}, u32[]{:S(2)}) %collective-permute-start.4) | collective-permute-done | bytes 262176 | tf_op jit(solution)/shard_map/ppermute | solution.py:394
  135.1 0.3 collective-permute-done.5.p3
  135.3 0.4 copy-done.1
  135.8 0.3 copy-done.2
  136.0 8.1 %make_delta.1 = (bf16[1024,2048]{1,0:T(8,128)(2,1)}, bf16[1024,256]{1,0:T(8,128)(2,1)}) custom-call(f32[512,128]{1,0:T(8,128)} %project.2.p0, f32[512,128]{1,0:T(8,128)} %copy-done, f32[512,128]{1,0:T(8,128)} %copy-done.1, f32[512,128]{1,0:T(8,128)} %copy-done.2, bf16[1024,256]{1,0:T(8,128)(2,1)} %broadcast_bitcast_fusion.ma_ref.mb_ref.mask_ref, ...), custom_call_target="tpu_custom_call" | custom-call | tf_op jit(solution)/shard_map/make_delta/pallas_call | solution.py:136
  144.1 11.1 %all-to-all-start.1 = ((bf16[128,8,2048]{2,1,0:T(8,128)(2,1)}), bf16[128,8,2048]{2,1,0:T(8,128)(2,1)}, u32[]{:S(2)}, u32[]{:S(2)}) async-start(bf16[128,8,2048]{2,1,0:T(8,128)(2,1)} %bitcast.36), calls=%async_computation.1 | async-start | bytes 8388608 | tf_op jit(solution)/shard_map/all_to_all | solution.py:496
  155.4 0.4 reshape.316
  155.8 1.1 constant_dynamic-slice_fusion.3
  156.9 1.0 collective-permute-start
  157.9 2.2 collective-permute-start.1
  160.1 1.5 collective-permute-start.2
  161.7 0.8 multiply_subtract_fusion
  162.5 0.8 dynamic_slice.30
  163.3 0.8 reshape_reshape.8.row_len_ref
  164.0 0.8 dynamic_slice.31
  164.9 0.8 reshape_reshape.9.row_prompt_ref
  165.7 0.7 sub.73.row_weight_ref
  166.5 0.6 and_select_fusion.3
  167.1 0.8 fusion.12
  168.0 81.2 %all-to-all-done.1.delta_hbm = bf16[128,8,2048]{2,1,0:T(8,128)(2,1)} async-done(((bf16[128,8,2048]{2,1,0:T(8,128)(2,1)}), bf16[128,8,2048]{2,1,0:T(8,128)(2,1)}, u32[]{:S(2)}, u32[]{:S(2)}) %all-to-all-start.1) | async-done | bytes 4194336 | tf_op jit(solution)/shard_map/all_to_all | solution.py:496
  249.1 14.3 %attend.1 = bf16[128,8,2048]{2,1,0:T(8,128)(2,1)} custom-call(s32[32]{0:T(128)} %copy-done.9, bf16[32,8,2048]{2,1,0:T(8,128)(2,1)} %bitcast.45, bf16[32,8,2048]{2,1,0:T(8,128)(2,1)} %bitcast.46, bf16[32,8,256]{2,1,0:T(8,128)(2,1)} %bitcast.50, bf16[32,8,256]{2,1,0:T(8,128)(2,1)} %bitcast.51, ...), custom_call_target="tpu_custom_call", output_to_operand_aliasing={{}: (12, {})} | custom-call | tf_op jit(solution)/shard_map/attend/pallas_call | solution.py:364
  263.5 102.4 %all_to_all.15 = bf16[128,8,2048]{2,1,0:T(8,128)(2,1)} all-to-all(bf16[128,8,2048]{2,1,0:T(8,128)(2,1)} %attend.1), channel_id=1, replica_groups=mesh['tok'=64,'kv'=4] {'tok'}, dimensions={0} | all-to-all | bytes 8388608 | tf_op jit(solution)/shard_map/all_to_all | solution.py:512
  365.9 6.4 %project.3.p0 = bf16[512,128]{1,0:T(8,128)(2,1)} custom-call(bf16[1024,2048]{1,0:T(8,128)(2,1)} %bitcast.33, bf16[1024,2048]{1,0:T(8,128)(2,1)} %bitcast.34, bf16[1024,256]{1,0:T(8,128)(2,1)} %broadcast_bitcast_fusion.ma_ref.mb_ref.mask_ref, bf16[1024,256]{1,0:T(8,128)(2,1)} %broadcast_bitcast_fusion.ma_ref.mb_ref.mask_ref, bf16[256,2048]{1,0:T(8,128)(2,1)} %bitcast.38), custom_call_target="tpu_custom_call" | custom-call | tf_op jit(solution)/shard_map/project/pallas_call | solution.py:88
  372.2 0.9 collective-permute-start.6
  373.1 2.1 collective-permute-start.7
  375.2 1.3 collective-permute-start.8
  376.5 5.0 %grad_up.1 = bf16[256,2048]{1,0:T(8,128)(2,1)} custom-call(bf16[1024,256]{1,0:T(8,128)(2,1)} %get-tuple-element.5.spread_ref, bf16[1024,2048]{1,0:T(8,128)(2,1)} %bitcast.35), custom_call_target="tpu_custom_call" | custom-call | tf_op jit(solution)/shard_map/grad_up/pallas_call | solution.py:173
  381.6 0.6 copy-done.5
  382.3 0.6 copy-done.7
  382.9 5.4 %grad_down.1 = bf16[256,2048]{1,0:T(8,128)(2,1)} custom-call(bf16[512,128]{1,0:T(8,128)(2,1)} %project.3.p0, bf16[512,128]{1,0:T(8,128)(2,1)} %copy-done.5, bf16[512,128]{1,0:T(8,128)(2,1)} %copy-done.6, bf16[512,128]{1,0:T(8,128)(2,1)} %copy-done.7, bf16[1024,256]{1,0:T(8,128)(2,1)} %broadcast_bitcast_fusion.ma_ref.mb_ref.mask_ref, ...), custom_call_target="tpu_custom_call" | custom-call | tf_op jit(solution)/shard_map/grad_down/pallas_call | solution.py:212
  (40 shorter events, 0.9 us)
Async XLA Ops:
  2.4 6.7 %copy-start.9 = (s32[32]{0:T(128)}, s32[32]{0:T(128)S(1)}, u32[]{:S(2)}) copy-start(s32[32]{0:T(128)S(1)} %get-tuple-element.13.target_ref) | copy-start | bytes 388
  9.1 12.7 %copy-start.8 = (s32[2048]{0:T(1024)S(1)}, s32[2048]{0:T(1024)}, u32[]{:S(2)}) copy-start(s32[2048]{0:T(1024)} %param.22) | copy-start | bytes 24580
  9.1 106.6 %all-to-all-start = ((bf16[128,8,2048]{2,1,0:T(8,128)(2,1)}), bf16[128,8,2048]{2,1,0:T(8,128)(2,1)}, u32[]{:S(2)}, u32[]{:S(2)}) async-start(bf16[128,8,2048]{2,1,0:T(8,128)(2,1)} %route_rows.1), calls=%async_computation | async-start | bytes 8388608 | tf_op jit(solution)/shard_map/all_to_all | solution.py:441
  122.1 6.6 %collective-permute-start.3 = (f32[512,128]{1,0:T(8,128)}, f32[512,128]{1,0:T(8,128)S(1)}, u32[]{:S(2)}, u32[]{:S(2)}) collective-permute-start(f32[512,128]{1,0:T(8,128)} %project.2.p0), channel_id=1, source_target_pairs={{0,1},{1,2},{2,3},{3,0},{4,5},{5,6},{6,7},{7,4},{8,9},{9,10},{10,1... | collective-permute-start | bytes 786440 | tf_op jit(solution)/shard_map/ppermute | solution.py:394
  123.3 11.7 %collective-permute-start.4 = (f32[512,128]{1,0:T(8,128)}, f32[512,128]{1,0:T(8,128)S(1)}, u32[]{:S(2)}, u32[]{:S(2)}) collective-permute-start(f32[512,128]{1,0:T(8,128)} %project.2.p0), channel_id=1, source_target_pairs={{0,2},{1,3},{2,0},{3,1},{4,6},{5,7},{6,4},{7,5},{8,10},{9,11},{10,... | collective-permute-start | bytes 786440 | tf_op jit(solution)/shard_map/ppermute | solution.py:394
  125.8 9.6 %collective-permute-start.5 = (f32[512,128]{1,0:T(8,128)}, f32[512,128]{1,0:T(8,128)S(1)}, u32[]{:S(2)}, u32[]{:S(2)}) collective-permute-start(f32[512,128]{1,0:T(8,128)} %project.2.p0), channel_id=1, source_target_pairs={{0,3},{1,0},{2,1},{3,2},{4,7},{5,4},{6,5},{7,6},{8,11},{9,8},{10,9... | collective-permute-start | bytes 786440 | tf_op jit(solution)/shard_map/ppermute | solution.py:394
  128.7 6.6 %copy-start = (f32[512,128]{1,0:T(8,128)}, f32[512,128]{1,0:T(8,128)S(1)}, u32[]{:S(2)}) copy-start(f32[512,128]{1,0:T(8,128)S(1)} %collective-permute-done.3.p1) | copy-start | bytes 786436
  135.1 0.7 copy-start.1
  135.3 0.7 copy-start.2
  144.1 11.2 %copy-start.3 = (bf16[2,64,1024]{2,1,0:T(8,128)(2,1)S(1)}, bf16[2,64,1024]{2,1,0:T(8,128)(2,1)}, u32[]{:S(2)}) copy-start(bf16[2,64,1024]{2,1,0:T(8,128)(2,1)} %param.19) | copy-start | bytes 786436
  144.1 11.2 %copy-start.4 = (bf16[2,64,1024]{2,1,0:T(8,128)(2,1)S(1)}, bf16[2,64,1024]{2,1,0:T(8,128)(2,1)}, u32[]{:S(2)}) copy-start(bf16[2,64,1024]{2,1,0:T(8,128)(2,1)} %param.18) | copy-start | bytes 786436
  144.1 105.0 %all-to-all-start.1 = ((bf16[128,8,2048]{2,1,0:T(8,128)(2,1)}), bf16[128,8,2048]{2,1,0:T(8,128)(2,1)}, u32[]{:S(2)}, u32[]{:S(2)}) async-start(bf16[128,8,2048]{2,1,0:T(8,128)(2,1)} %bitcast.36), calls=%async_computation.1 | async-start | bytes 8388608 | tf_op jit(solution)/shard_map/all_to_all | solution.py:496
  156.9 10.2 %collective-permute-start = (bf16[256,256]{1,0:T(8,128)(2,1)S(1)}, bf16[256,256]{1,0:T(8,128)(2,1)S(1)}, u32[]{:S(2)}, u32[]{:S(2)}) collective-permute-start(bf16[256,256]{1,0:T(8,128)(2,1)S(1)} %bitcast.52), channel_id=1, source_target_pairs={{0,1},{1,2},{2,3},{3,0},{4,5},{5,6},{6,7},{7,4},{8,9},{9,10},{10,1... | collective-permute-start | bytes 393224 | tf_op jit(solution)/shard_map/ppermute | solution.py:394
  157.9 9.2 %collective-permute-start.1 = (bf16[256,256]{1,0:T(8,128)(2,1)S(1)}, bf16[256,256]{1,0:T(8,128)(2,1)S(1)}, u32[]{:S(2)}, u32[]{:S(2)}) collective-permute-start(bf16[256,256]{1,0:T(8,128)(2,1)S(1)} %bitcast.53), channel_id=1, source_target_pairs={{0,2},{1,3},{2,0},{3,1},{4,6},{5,7},{6,4},{7,5},{8,10},{9,11},{10,... | collective-permute-start | bytes 393224 | tf_op jit(solution)/shard_map/ppermute | solution.py:394
  160.1 6.9 %collective-permute-start.2 = (bf16[256,256]{1,0:T(8,128)(2,1)S(1)}, bf16[256,256]{1,0:T(8,128)(2,1)S(1)}, u32[]{:S(2)}, u32[]{:S(2)}) collective-permute-start(bf16[256,256]{1,0:T(8,128)(2,1)S(1)} %bitcast.54), channel_id=1, source_target_pairs={{0,3},{1,0},{2,1},{3,2},{4,7},{5,4},{6,5},{7,6},{8,11},{9,8},{10,9... | collective-permute-start | bytes 393224 | tf_op jit(solution)/shard_map/ppermute | solution.py:394
  372.2 9.3 %collective-permute-start.6 = (bf16[512,128]{1,0:T(8,128)(2,1)}, bf16[512,128]{1,0:T(8,128)(2,1)S(1)}, u32[]{:S(2)}, u32[]{:S(2)}) collective-permute-start(bf16[512,128]{1,0:T(8,128)(2,1)} %project.3.p0), channel_id=1, source_target_pairs={{0,1},{1,2},{2,3},{3,0},{4,5},{5,6},{6,7},{7,4},{8,9},{9,10},{10,1... | collective-permute-start | bytes 393224 | tf_op jit(solution)/shard_map/ppermute | solution.py:394
  373.1 8.4 %collective-permute-start.7 = (bf16[512,128]{1,0:T(8,128)(2,1)}, bf16[512,128]{1,0:T(8,128)(2,1)S(1)}, u32[]{:S(2)}, u32[]{:S(2)}) collective-permute-start(bf16[512,128]{1,0:T(8,128)(2,1)} %project.3.p0), channel_id=1, source_target_pairs={{0,2},{1,3},{2,0},{3,1},{4,6},{5,7},{6,4},{7,5},{8,10},{9,11},{10,... | collective-permute-start | bytes 393224 | tf_op jit(solution)/shard_map/ppermute | solution.py:394
  375.2 6.3 %collective-permute-start.8 = (bf16[512,128]{1,0:T(8,128)(2,1)}, bf16[512,128]{1,0:T(8,128)(2,1)S(1)}, u32[]{:S(2)}, u32[]{:S(2)}) collective-permute-start(bf16[512,128]{1,0:T(8,128)(2,1)} %project.3.p0), channel_id=1, source_target_pairs={{0,3},{1,0},{2,1},{3,2},{4,7},{5,4},{6,5},{7,6},{8,11},{9,8},{10,9... | collective-permute-start | bytes 393224 | tf_op jit(solution)/shard_map/ppermute | solution.py:394
  381.6 0.7 copy-start.5
  381.6 0.7 copy-start.6
  382.3 0.6 copy-start.7
